TPU v7x, 32 devices: a whole 2x2x4 slice. The times are simulated.
32 devices in a mesh: ep: 8 (over z, x), tp: 4 (over y, core).
Axes of the slice: x: 2, y: 2, z: 4, core: 2. Of those that a mesh axis runs over, the one named last changes fastest.
Arguments:
- hidden_in: bfloat16 [2048, 3584], P('ep', 'tp'), may hold values from -6 to 6
- moe_gain: bfloat16 [3584], replicated, may hold values from 0.099609375 to 1.8984375
- router_weight: bfloat16 [3584, 256], P('tp'), may hold values from -0.09375 to 0.09375
- expert_ids: int32 [2048, 8], P('ep'), may hold values from 0 to 255, all different within a row; in each aligned block of 256 rows (0 to 255, 256 to 511, ...) at most 16 rows name the same one
- shared_gate: bfloat16 [3584, 1024], P(None, 'tp'), may hold values from -0.09375 to 0.09375
- shared_up: bfloat16 [3584, 1024], P(None, 'tp'), may hold values from -0.09375 to 0.09375
- shared_down: bfloat16 [1024, 3584], P('tp'), may hold values from -0.1875 to 0.1875
- expert_gate: bfloat16 [8, 3584, 1024], P('ep', None, 'tp'), may hold values from -0.09375 to 0.09375
- expert_up: bfloat16 [8, 3584, 1024], P('ep', None, 'tp'), may hold values from -0.09375 to 0.09375
- expert_down: bfloat16 [8, 1024, 3584], P('ep', 'tp'), may hold values from -0.1875 to 0.1875
- attn_gain: bfloat16 [3584], P('tp'), may hold values from 0.099609375 to 1.8984375
- kv_down: bfloat16 [3584, 576], P('tp'), may hold values from -0.09375 to 0.09375
- kv_gain: bfloat16 [512], replicated, may hold values from 0.099609375 to 1.8984375
- doc_lengths: int32 [8, 4], P('ep'), may hold values from 1 to 128, 256 in all within a row
- page_table: int32 [8, 4], P('ep'), may hold values from 0 to 3, each once within a row
Outputs:
- layer_out: bfloat16 [2048, 3584], P('ep', 'tp')
- kv_pages: bfloat16 [8, 4, 64, 576], P('ep', 'tp')
Inputs may be any that keep to these rules, and one draw needn't show every extreme that they name: `expert_ids`: each row names 8 different experts. Among the rows of one ep index no expert is named more than 16 times. `doc_lengths`: each row sums to 256. `page_table`: each row holds every number below 4 once.
All inputs are finite; a program needn't handle non-finite values.
Results may differ from a plain program's by a relative error of at most 0.0065.
Values may be sent and summed in bfloat16 or wider, within the bound.
No kernel may reach another device: no remote copies, remote signals or barrier semaphores. Data moves between devices by JAX's collectives and lax.ppermute only.
A program may use at most 128 MiB of HBM per device.

v0:
```python
import jax
import jax.numpy as jnp
from jax import lax
from jax.sharding import PartitionSpec as P

CAP = 16
KVR = 512
EPS = 1e-06
ROUTE_SCALE = 2.5
THETA = 10000.0


def silu(values):
    return values / (1.0 + jnp.exp(-values))


def route_weights(logits, expert_ids):
    scores = 1.0 / (1.0 + jnp.exp(-logits))
    picked = jnp.take_along_axis(scores, expert_ids, axis=1)
    return ROUTE_SCALE * picked / jnp.sum(picked, axis=1, keepdims=True)


def slot_table(expert_ids, gate_weights, expert_count, capacity):
    token_count = expert_ids.shape[0]
    columns = jnp.arange(expert_count, dtype=jnp.int32)
    matched = expert_ids[:, :, None] == columns[None, None, :]
    weight_rows = jnp.sum(jnp.where(matched, gate_weights[:, :, None], 0.0), axis=1)
    chosen = jnp.any(matched, axis=1).astype(jnp.int32)
    before = jnp.cumsum(chosen, axis=0) - chosen
    target = jnp.where(chosen > 0, columns[None, :] * capacity + before, expert_count * capacity)
    token_index = jnp.broadcast_to(jnp.arange(token_count, dtype=jnp.int32)[:, None], target.shape)
    slot_token = (
        jnp.full((expert_count * capacity + 1,), token_count, jnp.int32)
        .at[target.reshape(-1)]
        .set(token_index.reshape(-1))
    )
    slot_weight = (
        jnp.zeros((expert_count * capacity + 1,), jnp.float32)
        .at[target.reshape(-1)]
        .set(weight_rows.reshape(-1))
    )
    return (slot_token[:-1], slot_weight[:-1])


def positions_of(lengths, token_count):
    doc_ends = jnp.cumsum(lengths)
    doc_starts = doc_ends - lengths
    token_index = jnp.arange(token_count, dtype=jnp.int32)
    doc_begin = jnp.max(
        jnp.where(doc_starts[None, :] <= token_index[:, None], doc_starts[None, :], 0), axis=1
    )
    return (token_index - doc_begin).astype(jnp.float32)


def rotate(rope_part, position):
    half_width = rope_part.shape[1] // 2
    frequency = THETA ** (-jnp.arange(half_width, dtype=jnp.float32) * 2.0 / rope_part.shape[1])
    angles = position[:, None] * frequency[None, :]
    cosine = jnp.cos(angles)
    sine_part = jnp.sin(angles)
    first_half = rope_part[:, :half_width]
    second_half = rope_part[:, half_width:]
    return jnp.concatenate(
        [
            first_half * cosine - second_half * sine_part,
            second_half * cosine + first_half * sine_part,
        ],
        axis=1,
    )


def finish(latent, position, kv_gain):
    plain_part = latent[:, :KVR]
    row_scale = lax.rsqrt(jnp.mean(plain_part * plain_part, axis=1, keepdims=True) + EPS)
    normed = plain_part * row_scale * kv_gain.astype(jnp.float32)
    return jnp.concatenate([normed, rotate(latent[:, KVR:], position)], axis=1).astype(jnp.bfloat16)


def per_device(
    hidden_in,
    moe_gain,
    router_weight,
    expert_ids,
    shared_gate,
    shared_up,
    shared_down,
    expert_gate,
    expert_up,
    expert_down,
    attn_gain,
    kv_down,
    kv_gain,
    doc_lengths,
    page_table,
):
    groups = lax.axis_size("ep")
    tp_count = lax.axis_size("tp")
    member = lax.axis_index("tp")
    tok_rows, width_local = hidden_in.shape
    full_width = width_local * tp_count
    capacity = CAP
    gathered = lax.all_gather(hidden_in, "tp", axis=1, tiled=True)
    stream = gathered.astype(jnp.float32)
    inverse = lax.rsqrt(jnp.mean(stream * stream, axis=1, keepdims=True) + EPS)
    normed = (stream * inverse * moe_gain.astype(jnp.float32)).astype(jnp.bfloat16)
    normed_local = lax.dynamic_slice_in_dim(normed, member * width_local, width_local, 1)
    logits = lax.psum(
        jnp.dot(normed_local, router_weight, preferred_element_type=jnp.float32).astype(
            jnp.bfloat16
        ),
        "tp",
    ).astype(jnp.float32)
    gate_weights = route_weights(logits, expert_ids)
    slot_token, slot_weight = slot_table(expert_ids, gate_weights, groups, capacity)
    shared_hidden = (
        silu(jnp.dot(normed, shared_gate, preferred_element_type=jnp.float32))
        * jnp.dot(normed, shared_up, preferred_element_type=jnp.float32)
    ).astype(jnp.bfloat16)
    shared_part = jnp.dot(shared_hidden, shared_down, preferred_element_type=jnp.float32)
    w_gate = expert_gate[0]
    w_up = expert_up[0]
    w_down = expert_down[0]
    padded = jnp.concatenate([normed, jnp.zeros((1, full_width), jnp.bfloat16)], axis=0)
    send_rows = padded[slot_token].reshape(groups, capacity, full_width)
    arrived_block = lax.all_to_all(send_rows, "ep", split_axis=0, concat_axis=0, tiled=True)
    flat_rows = arrived_block.reshape(-1, full_width)
    hidden_rows = (
        silu(jnp.dot(flat_rows, w_gate, preferred_element_type=jnp.float32))
        * jnp.dot(flat_rows, w_up, preferred_element_type=jnp.float32)
    ).astype(jnp.bfloat16)
    result = jnp.dot(hidden_rows, w_down, preferred_element_type=jnp.float32)
    outputs = result.reshape(arrived_block.shape[0], arrived_block.shape[1], full_width)
    reduced = lax.psum_scatter(outputs, "tp", scatter_dimension=2, tiled=True)
    returned = lax.all_to_all(reduced, "ep", split_axis=0, concat_axis=0, tiled=True)
    weighted = returned.reshape(groups * capacity, width_local) * slot_weight[:, None]
    routed = jax.ops.segment_sum(weighted, slot_token, num_segments=tok_rows + 1)[:tok_rows]
    branch_sum = lax.psum_scatter(shared_part, "tp", scatter_dimension=1, tiled=True) + routed
    layer_out = (hidden_in.astype(jnp.float32) + branch_sum).astype(jnp.bfloat16)
    out_values = layer_out.astype(jnp.float32)
    scaled = (out_values * attn_gain.astype(jnp.float32)).astype(jnp.bfloat16)
    latent_part = jnp.dot(scaled, kv_down, preferred_element_type=jnp.float32)
    squares = jnp.sum(out_values * out_values, axis=1)
    positions = positions_of(doc_lengths[0], tok_rows)
    page_count = page_table.shape[1]
    per_owner = page_count // tp_count
    page_len = tok_rows // page_count
    own_slots = lax.dynamic_slice_in_dim(page_table[0], member * per_owner, per_owner, 0)
    latent_sum, energy = lax.psum((latent_part, squares), "tp")
    latent = latent_sum * lax.rsqrt(energy / full_width + EPS)[:, None]
    row_index = (
        own_slots[:, None] * page_len + jnp.arange(page_len, dtype=jnp.int32)[None, :]
    ).reshape(-1)
    cache_rows = finish(latent[row_index], positions[row_index], kv_gain)
    page_out = cache_rows.reshape(1, per_owner, page_len, cache_rows.shape[-1])
    return (layer_out, page_out)


def solution(mesh):
    placed = (
        P("ep", "tp"),
        P(),
        P("tp", None),
        P("ep", None),
        P(None, "tp"),
        P(None, "tp"),
        P("tp", None),
        P("ep", None, "tp"),
        P("ep", None, "tp"),
        P("ep", "tp", None),
        P("tp"),
        P("tp", None),
        P(),
        P("ep", None),
        P("ep", None),
    )
    return jax.shard_map(
        per_device,
        mesh=mesh,
        in_specs=placed,
        out_specs=(P("ep", "tp"), P("ep", "tp", None, None)),
        check_vma=False,
    )
```

profile of v0, /device:TPU:0, one launch (start us, length us, event | category | flops | bytes accessed | tf_op | source)
XLA Modules:
  0.0 229.4 jit_solution(17543167574252839877)
XLA Ops:
  7.2 0.0 all-gather.2.cloned.1.call-start
  7.2 0.7 all-gather.2.cloned.1.call-update
  7.9 0.0 reduce-scatter.5.cloned.1.call-start
  8.0 0.7 fusion.33
  8.7 0.6 reduce-window.9
  9.3 0.2 slice_reduce_fusion
  9.5 0.7 convert_element_type.59
  10.2 0.1 fusion.45
  10.3 0.1 copy.34
  10.5 0.1 reshape.197
  10.6 0.1 reshape.239
  10.7 8.0 %scatter_custom_fusion = s32[129]{0:T(256)S(1)} fusion(s32[2048]{0:T(1024)S(1)} %bitcast.59, s32[2048]{0:T(1024)S(1)} %reshape.239, s32[]{:T(128)} %constant.28.clone.1), kind=kCustom, calls=%fused_computation.93 | custom fusion | bytes 520 | tf_op jit(solution)/shard_map/scatter | solution.py:35
  18.8 14.7 %all-gather.2.cloned.1.call-done = bf16[256,3584]{1,0:T(8,128)(2,1)} async-done(((bf16[256,896]{1,0:T(8,128)(2,1)}), bf16[256,3584]{1,0:T(8,128)(2,1)}) %all-gather.2.cloned.1.call-update) | async-done | bytes 1835024 | tf_op jit(solution)/shard_map/all_gather | solution.py:102
  33.4 2.1 fusion
  35.5 0.5 fusion.2
  36.1 1.2 copy-done.1
  37.3 1.4 concatenate.20
  38.7 3.8 %gather_fusion = bf16[128,3584]{1,0:T(8,128)(2,1)S(1)} fusion(bf16[257,3584]{1,0:T(8,128)(2,1)} %concatenate.20, s32[1024]{0:T(1024)S(1)} %pad_clamp_fusion.1), kind=kCustom, calls=%fused_computation | custom fusion | bytes 1835520 | tf_op jit(solution)/shard_map/gather | solution.py:124
  42.5 29.1 %all_to_all.10 = bf16[8,16,3584]{2,1,0:T(8,128)(2,1)S(1)} all-to-all(bf16[8,16,3584]{2,1,0:T(8,128)(2,1)S(1)} %bitcast.57), channel_id=1, replica_groups=mesh['ep'=8,'tp'=4] {'ep'}, dimensions={0} | all-to-all | bytes 1835008 | tf_op jit(solution)/shard_map/all_to_all | solution.py:125
  71.7 0.4 fusion.7
  72.1 1.1 copy-done.6
  73.2 0.4 fusion.14
  73.6 1.1 copy-done.3
  74.7 1.7 fusion.3
  76.4 0.0 all-reduce.4.cloned.1.call-start
  76.4 0.9 copy-done.9
  77.4 2.0 convolution_convert_fusion
  79.4 2.8 %fusion.56 = f32[256,256]{1,0:T(8,128)S(1)} fusion(bf16[256,3584]{1,0:T(8,128)(2,1)} %copy-done.1, bf16[3584,256]{1,0:T(8,128)(2,1)} %param.19), kind=kOutput, calls=%fused_computation.97 | convolution fusion | flops 469762048 | bytes 3932160 | tf_op jit(solution)/shard_map/dot_general | solution.py:116
  82.2 0.0 reduce-scatter.3.cloned.1.call-start
  82.2 6.1 %fusion.13 = f32[256,3584]{1,0:T(8,128)} fusion(bf16[256,3584]{1,0:T(8,128)(2,1)S(1)} %copy-done, bf16[256,3584]{1,0:T(8,128)(2,1)} %copy-done.1, bf16[3584,256]{1,0:T(8,128)(2,1)} %param.20, f32[256,256]{1,0:T(8,128)S(1)} %fusion.56), kind=kOutput, calls=%fused_computation.24 | convolution fusion | flops 939851776 | bytes 9437184 | tf_op jit(solution)/shard_map/dot_general | solution.py:119
  88.4 0.6 copy-done.14
  89.0 0.2 reduce-window_2_clone.1
  89.2 0.6 fusion.55
  89.7 0.1 select_reduce_fusion.1
  89.9 14.1 %reduce-scatter.5.cloned.1.call-done = f32[8,16,896]{2,1,0:T(8,128)} async-done(((f32[8,16,3584]{2,1,0:T(8,128)}), f32[8,16,896]{2,1,0:T(8,128)}) %reduce-scatter.5.cloned.1.call-update) | async-done | bytes 458768 | tf_op jit(solution)/shard_map/reduce_scatter | solution.py:133
  103.9 5.5 %all-to-all-start.1 = ((f32[8,16,896]{2,1,0:T(8,128)}), f32[8,16,896]{2,1,0:T(8,128)S(1)}, u32[]{:S(2)}, u32[]{:S(2)}) async-start(f32[8,16,896]{2,1,0:T(8,128)} %reduce-scatter.5.cloned.1.call-done), calls=%async_computation.3 | async-start | bytes 917504 | tf_op jit(solution)/shard_map/all_to_all | solution.py:134
  109.4 0.0 all-reduce.6.cloned.1.call-start
  109.5 0.7 fusion.47
  110.2 0.1 copy.35
  110.3 0.1 reshape.229
  110.4 0.8 gather_fusion.2
  111.2 27.4 %all-reduce.4.cloned.1.call-done = bf16[256,256]{1,0:T(8,128)(2,1)} async-done(((bf16[256,256]{1,0:T(8,128)(2,1)}), bf16[256,256]{1,0:T(8,128)(2,1)}) %all-reduce.4.cloned.1.call-update) | async-done | bytes 131088 | tf_op jit(solution)/shard_map/psum | solution.py:107
  138.6 1.0 add_divide_fusion
  139.6 16.6 %gather_fusion.3 = f32[2048]{0:T(1024)S(1)} fusion(f32[256,256]{1,0:T(8,128)S(1)} %add_divide_fusion, s32[2048]{0:T(1024)S(1)} %reshape.229), kind=kCustom, calls=%fused_computation.3 | custom fusion | bytes 32768 | tf_op jit(solution)/shard_map/jit(take_along_axis)/gather | solution.py:19
  156.2 0.1 reshape.232
  156.4 0.1 copy.36
  156.5 0.1 copy.37
  156.6 0.1 reshape.247
  156.7 8.0 %scatter_custom_fusion.1 = f32[129]{0:T(256)S(1)} fusion(s32[2048]{0:T(1024)S(1)} %bitcast.60, f32[2048]{0:T(1024)S(1)} %reshape.247, f32[]{:T(128)} %constant.24.clone.1), kind=kCustom, calls=%fused_computation.88 | custom fusion | bytes 520 | tf_op jit(solution)/shard_map/scatter | solution.py:40
  164.8 0.9 bitcast_multiply_fusion
  165.7 2.3 %scatter_custom_fusion.2 = f32[257,896]{1,0:T(8,128)S(1)} fusion(s32[128]{0:T(128)S(1)} %get-tuple-element.7, f32[128,896]{1,0:T(8,128)} %bitcast_multiply_fusion, f32[]{:T(128)} %constant.24.clone.1), kind=kCustom, calls=%fused_computation.31 | custom fusion | flops 114688 | bytes 921600 | tf_op jit(solution)/shard_map/scatter-add | solution.py:136
  168.0 14.1 %reduce-scatter.3.cloned.1.call-done = f32[256,896]{1,0:T(8,128)} async-done(((f32[256,3584]{1,0:T(8,128)}), f32[256,896]{1,0:T(8,128)}) %reduce-scatter.3.cloned.1.call-update) | async-done | bytes 917520 | tf_op jit(solution)/shard_map/reduce_scatter | solution.py:137
  182.1 1.5 fusion.18
  183.7 0.8 copy-done.7
  184.4 1.3 fusion.23
  185.8 5.8 %psum.23 = f32[256]{0:T(256)S(1)} all-reduce(f32[256]{0:T(256)S(1)} %get-tuple-element.2), channel_id=1, replica_groups=mesh['ep'=8,'tp'=4] {'tp'}, use_global_device_ids=true, to_apply=%region_14.15 | all-reduce | flops 256 | bytes 2048 | tf_op jit(solution)/shard_map/psum | solution.py:148
  191.6 28.2 %all-reduce.6.cloned.1.call-done = f32[256,576]{0,1:T(8,128)} async-done(((f32[256,576]{0,1:T(8,128)}), f32[256,576]{0,1:T(8,128)}) %all-reduce.6.cloned.1.call-update) | async-done | bytes 589840 | tf_op jit(solution)/shard_map/psum | solution.py:148
  219.7 1.1 broadcast_multiply_fusion
  220.8 0.2 copy.38
  221.1 0.7 gather_fusion.1
  221.8 0.1 multiply_reduce_fusion
  221.9 0.2 fusion.43
  222.1 0.1 fusion.32
  222.2 0.7 pad_maximum_fusion
  (51 shorter events, 0.3 us)
Async XLA Ops:
  7.2 75.1 %copy-start = (bf16[256,3584]{1,0:T(8,128)(2,1)S(1)}, bf16[256,3584]{1,0:T(8,128)(2,1)}, u32[]{:S(2)}) copy-start(bf16[256,3584]{1,0:T(8,128)(2,1)} %param.21) | copy-start | bytes 5505028
  7.2 26.3 %all-gather.2.cloned.1.call-start = ((), (), s32[]{:S(2)}) async-start(), calls=%async_computation.4 | async-start | bytes 2293760 | tf_op jit(solution)/shard_map/all_gather | solution.py:102
  7.9 96.0 %reduce-scatter.5.cloned.1.call-start = ((), (), s32[]{:S(2)}) async-start(), calls=%async_computation.6 | async-start | bytes 2293760 | tf_op jit(solution)/shard_map/reduce_scatter | solution.py:133
  33.4 2.1 copy-start.2
  36.1 1.3 copy-start.1
  42.5 29.1 %copy-start.5 = (bf16[1,3584,256]{2,1,0:T(8,128)(2,1)S(1)}, bf16[1,3584,256]{2,1,0:T(8,128)(2,1)}, u32[]{:S(2)}) copy-start(bf16[1,3584,256]{2,1,0:T(8,128)(2,1)} %param.22) | copy-start | bytes 5505028
  71.7 1.5 copy-start.6
  73.2 1.5 copy-start.3
  76.4 1.0 copy-start.9
  76.4 62.2 %all-reduce.4.cloned.1.call-start = ((), (), s32[]{:S(2)}) async-start(), calls=%async_computation.7 | async-start | bytes 262144 | tf_op jit(solution)/shard_map/psum | solution.py:107
  82.2 99.9 %reduce-scatter.3.cloned.1.call-start = ((), (), s32[]{:S(2)}) async-start(), calls=%async_computation.5 | async-start | bytes 4587520 | tf_op jit(solution)/shard_map/reduce_scatter | solution.py:137
  88.3 0.7 copy-start.14
  88.3 0.8 copy-start.13
  88.3 1.5 copy-start.10
  88.3 21.8 %copy-start.12 = (bf16[512]{0:T(512)(128)(2,1)S(1)}, bf16[512]{0:T(512)(128)(2,1)}, u32[]{:S(2)}) copy-start(bf16[512]{0:T(512)(128)(2,1)} %param.27) | copy-start | bytes 3076
  88.3 21.8 %copy-start.11 = (bf16[896]{0:T(1024)(128)(2,1)S(1)}, bf16[896]{0:T(1024)(128)(2,1)}, u32[]{:S(2)}) copy-start(bf16[896]{0:T(1024)(128)(2,1)} %param.25) | copy-start | bytes 5380
  103.9 60.9 %all-to-all-start.1 = ((f32[8,16,896]{2,1,0:T(8,128)}), f32[8,16,896]{2,1,0:T(8,128)S(1)}, u32[]{:S(2)}, u32[]{:S(2)}) async-start(f32[8,16,896]{2,1,0:T(8,128)} %reduce-scatter.5.cloned.1.call-done), calls=%async_computation.3 | async-start | bytes 917504 | tf_op jit(solution)/shard_map/all_to_all | solution.py:134
  109.4 110.3 %all-reduce.6.cloned.1.call-start = ((), (), s32[]{:S(2)}) async-start(), calls=%async_computation.8 | async-start | bytes 1179648 | tf_op jit(solution)/shard_map/psum | solution.py:148
  156.2 25.9 %copy-start.4 = (bf16[256,896]{1,0:T(8,128)(2,1)S(1)}, bf16[256,896]{1,0:T(8,128)(2,1)}, u32[]{:S(2)}) copy-start(bf16[256,896]{1,0:T(8,128)(2,1)} %param.15) | copy-start | bytes 1376260
  182.1 2.3 %copy-start.8 = (bf16[896,576]{0,1:T(8,128)(2,1)S(1)}, bf16[896,576]{0,1:T(8,128)(2,1)}, u32[]{:S(2)}) copy-start(bf16[896,576]{0,1:T(8,128)(2,1)} %param.26) | copy-start | bytes 3096580
  183.7 0.8 copy-start.7
Sparse Core Ops, SparseCore 0:
  9.6 23.8 all-gather.1
  76.5 27.3 reduce-scatter.4
  106.8 31.7 all-reduce.3
  141.0 41.0 reduce-scatter.2
  185.9 33.7 all-reduce.5
where the time goes:
time: 230 us; the launch traced here: 229 us
  waiting for transfers between devices  99.2 us (43%)
  local copies, waits for them, and re-layouts  46.6 us (20%)
  blocking collectives  34.9 us (15%)
  matrix products  14.7 us (6%)
  other arithmetic  14.3 us (6%)
  between operations  14.1 us (6%)
  starting transfers between devices  5.7 us (2%)
    all_to_all x1, blocking collectives, per_device(): lax.all_to_all(send_rows, 'ep', split_axis=0, concat_axis=0, tiled=True)  29.1 us
    psum x1, waiting for transfers between devices, per_device(): latent_sum, energy = lax.psum((latent_part, squares), 'tp')  28.2 us
    psum x1, waiting for transfers between devices, per_device(): lax.psum(jnp.dot(normed_local, router_weight, preferred_element_type=jnp....  27.4 us
    gather x5, local copies, waits for them, and re-layouts, route_weights(): picked = jnp.take_along_axis(scores, expert_ids, axis=1)  17 us
    all_gather x1, waiting for transfers between devices, per_device(): gathered = lax.all_gather(hidden_in, 'tp', axis=1, tiled=True)  14.7 us
    reduce_scatter x1, waiting for transfers between devices, per_device(): lax.psum_scatter(shared_part, 'tp', scatter_dimension=1, tiled=True)  14.1 us
    reduce_scatter x1, waiting for transfers between devices, per_device(): reduced = lax.psum_scatter(outputs, 'tp', scatter_dimension=2, tiled=True)  14.1 us
    scatter x1, local copies, waits for them, and re-layouts, slot_table(): slot_weight = jnp.zeros((expert_count * capacity + 1,), jnp.float32).at[t...  8.04 us
  transfers between devices with their start and end apart: 6, of which 5 were waited for; matrix products, arithmetic and copies ran while one was open for 23% of the time, Pallas kernels for 0%

commit v1 on v0

--- a/solution.py
+++ b/solution.py
@@ -104,11 +104,14 @@
     inverse = lax.rsqrt(jnp.mean(stream * stream, axis=1, keepdims=True) + EPS)
     normed = (stream * inverse * moe_gain.astype(jnp.float32)).astype(jnp.bfloat16)
     normed_local = lax.dynamic_slice_in_dim(normed, member * width_local, width_local, 1)
-    logits = lax.psum(
-        jnp.dot(normed_local, router_weight, preferred_element_type=jnp.float32).astype(
-            jnp.bfloat16
+    logits = jnp.sum(
+        lax.all_gather(
+            jnp.dot(normed_local, router_weight, preferred_element_type=jnp.float32).astype(
+                jnp.bfloat16
+            ),
+            "tp",
         ),
-        "tp",
+        axis=0,
     ).astype(jnp.float32)
     gate_weights = route_weights(logits, expert_ids)
     slot_token, slot_weight = slot_table(expert_ids, gate_weights, groups, capacity)

time: 230 us -> 196 us (0.85)
  waiting for transfers between devices: 99.2 us -> 59.5 us
  blocking collectives: 34.9 us -> 41.4 us
    psum x1 -> x0, waiting for transfers between devices: 27.4 us -> none  [per_device(): lax.psum(jnp.dot(normed_local, router_weight, preferred_element_type=jnp....]
    reduce_scatter x1, waiting for transfers between devices: 14.1 us -> 1.87 us  [per_device(): lax.psum_scatter(shared_part, 'tp', scatter_dimension=1, tiled=True)]
    all_gather x0 -> x1, blocking collectives: none -> 6.5 us  [per_device(): lax.all_gather(jnp.dot(normed_local, router_weight, preferred_element_typ...]
  transfers between devices with their start and end apart: 6 -> 5, of which waited for: 5 -> 4; matrix products, arithmetic and copies ran while one was open for 23% -> 27% of each run, Pallas kernels for 0% -> 0%
where the time goes in v1:
time: 196 us; the launch traced here: 195 us
  waiting for transfers between devices  59.5 us (30%)
  local copies, waits for them, and re-layouts  45.8 us (23%)
  blocking collectives  41.4 us (21%)
  other arithmetic  14.5 us (7%)
  between operations  14.1 us (7%)
  matrix products  13.9 us (7%)
  starting transfers between devices  5.68 us (3%)
    all_to_all x1, blocking collectives, per_device(): lax.all_to_all(send_rows, 'ep', split_axis=0, concat_axis=0, tiled=True)  29.1 us
    psum x1, waiting for transfers between devices, per_device(): latent_sum, energy = lax.psum((latent_part, squares), 'tp')  28.2 us
    gather x5, local copies, waits for them, and re-layouts, route_weights(): picked = jnp.take_along_axis(scores, expert_ids, axis=1)  17 us
    all_gather x1, waiting for transfers between devices, per_device(): gathered = lax.all_gather(hidden_in, 'tp', axis=1, tiled=True)  14.7 us
    reduce_scatter x1, waiting for transfers between devices, per_device(): reduced = lax.psum_scatter(outputs, 'tp', scatter_dimension=2, tiled=True)  14.1 us
    scatter x1, local copies, waits for them, and re-layouts, slot_table(): slot_weight = jnp.zeros((expert_count * capacity + 1,), jnp.float32).at[t...  8.22 us
    scatter x1, local copies, waits for them, and re-layouts, slot_table(): slot_token = jnp.full((expert_count * capacity + 1,), token_count, jnp.in...  8.04 us
    all_gather x1, blocking collectives, per_device(): lax.all_gather(jnp.dot(normed_local, router_weight, preferred_element_typ...  6.5 us
  transfers between devices with their start and end apart: 5, of which 4 were waited for; matrix products, arithmetic and copies ran while one was open for 27% of the time, Pallas kernels for 0%

profile of v1, /device:TPU:0, one launch (start us, length us, event | category | flops | bytes accessed | tf_op | source)
XLA Modules:
  0.0 194.9 jit_solution(14917667111120966947)
XLA Ops:
  7.2 0.0 all-gather.3.cloned.1.call-start
  7.2 0.7 all-gather.3.cloned.1.call-update
  7.9 0.0 reduce-scatter.5.cloned.1.call-start
  8.0 0.7 fusion.33
  8.7 0.6 reduce-window.9
  9.3 0.2 slice_reduce_fusion
  9.5 0.7 convert_element_type.61
  10.2 0.1 fusion.45
  10.3 0.1 copy.34
  10.5 0.1 reshape.197
  10.6 0.1 reshape.239
  10.7 8.0 %scatter_custom_fusion = s32[129]{0:T(256)S(1)} fusion(s32[2048]{0:T(1024)S(1)} %bitcast.61, s32[2048]{0:T(1024)S(1)} %reshape.239, s32[]{:T(128)} %constant.28.clone.1), kind=kCustom, calls=%fused_computation.93 | custom fusion | bytes 520 | tf_op jit(solution)/shard_map/scatter | solution.py:35
  18.8 14.7 %all-gather.3.cloned.1.call-done = bf16[256,3584]{1,0:T(8,128)(2,1)} async-done(((bf16[256,896]{1,0:T(8,128)(2,1)}), bf16[256,3584]{1,0:T(8,128)(2,1)}) %all-gather.3.cloned.1.call-update) | async-done | bytes 1835024 | tf_op jit(solution)/shard_map/all_gather | solution.py:102
  33.4 2.1 %fusion = f32[256]{0:T(256)S(1)} fusion(bf16[256,3584]{1,0:T(8,128)(2,1)} %all-gather.3.cloned.1.call-done), kind=kLoop, calls=%fused_computation.9 | loop fusion | flops 2752256 | bytes 1836032 | tf_op jit(solution)/shard_map/reduce_sum | solution.py:104
  35.5 0.5 fusion.2
  36.1 1.2 copy-done.1
  37.3 1.4 concatenate.20
  38.7 3.8 %gather_fusion = bf16[128,3584]{1,0:T(8,128)(2,1)S(1)} fusion(bf16[257,3584]{1,0:T(8,128)(2,1)} %concatenate.20, s32[1024]{0:T(1024)S(1)} %pad_clamp_fusion.1), kind=kCustom, calls=%fused_computation | custom fusion | bytes 1835520 | tf_op jit(solution)/shard_map/gather | solution.py:127
  42.5 29.1 %all_to_all.10 = bf16[8,16,3584]{2,1,0:T(8,128)(2,1)S(1)} all-to-all(bf16[8,16,3584]{2,1,0:T(8,128)(2,1)S(1)} %bitcast.58), channel_id=1, replica_groups=mesh['ep'=8,'tp'=4] {'ep'}, dimensions={0} | all-to-all | bytes 1835008 | tf_op jit(solution)/shard_map/all_to_all | solution.py:128
  71.7 0.4 fusion.7
  72.1 1.1 copy-done.6
  73.2 0.4 fusion.14
  73.6 1.1 copy-done.3
  74.7 1.7 fusion.3
  76.4 0.0 reduce-scatter.3.cloned.1.call-start
  76.4 2.7 %fusion.56 = f32[256,256]{1,0:T(8,128)S(1)} fusion(bf16[256,3584]{1,0:T(8,128)(2,1)} %copy-done.1, bf16[3584,256]{1,0:T(8,128)(2,1)} %param.19), kind=kOutput, calls=%fused_computation.97 | convolution fusion | flops 469762048 | bytes 3932160 | tf_op jit(solution)/shard_map/dot_general | solution.py:119
  79.1 6.0 %fusion.13 = f32[256,3584]{1,0:T(8,128)} fusion(bf16[256,3584]{1,0:T(8,128)(2,1)S(1)} %copy-done, bf16[256,3584]{1,0:T(8,128)(2,1)} %copy-done.1, bf16[3584,256]{1,0:T(8,128)(2,1)} %param.20, f32[256,256]{1,0:T(8,128)S(1)} %fusion.56), kind=kOutput, calls=%fused_computation.24 | convolution fusion | flops 939851776 | bytes 9437184 | tf_op jit(solution)/shard_map/dot_general | solution.py:122
  85.2 0.0 reduce-scatter.3.cloned.1.call-update
  85.2 0.6 copy-done.14
  85.8 0.2 reduce-window_2_clone.1
  86.1 0.1 copy.35
  86.2 0.1 reshape.229
  86.3 0.6 fusion.55
  86.9 0.6 fusion.47
  87.6 0.1 select_reduce_fusion.1
  87.7 0.8 gather_fusion.2
  88.5 1.3 convolution_convert_fusion
  89.8 14.1 %reduce-scatter.5.cloned.1.call-done = f32[8,16,896]{2,1,0:T(8,128)} async-done(((f32[8,16,3584]{2,1,0:T(8,128)}), f32[8,16,896]{2,1,0:T(8,128)}) %reduce-scatter.5.cloned.1.call-update) | async-done | bytes 458768 | tf_op jit(solution)/shard_map/reduce_scatter | solution.py:136
  103.9 5.5 %all-to-all-start.1 = ((f32[8,16,896]{2,1,0:T(8,128)}), f32[8,16,896]{2,1,0:T(8,128)}, u32[]{:S(2)}, u32[]{:S(2)}) async-start(f32[8,16,896]{2,1,0:T(8,128)} %reduce-scatter.5.cloned.1.call-done), calls=%async_computation.3 | async-start | bytes 917504 | tf_op jit(solution)/shard_map/all_to_all | solution.py:137
  109.4 0.0 all-reduce.3.cloned.1.call-start
  109.4 6.5 %all-gather = bf16[1024,256]{1,0:T(8,128)(2,1)S(1)} all-gather(bf16[256,256]{1,0:T(8,128)(2,1)S(1)} %convolution_convert_fusion), channel_id=2, replica_groups=mesh['ep'=8,'tp'=4] {'tp'}, dimensions={0}, use_global_device_ids=true | all-gather | bytes 655360 | tf_op jit(solution)/shard_map/all_gather | solution.py:108
  115.9 0.1 reduce_sum.58
  116.0 0.1 add_divide_fusion
  116.1 16.6 %gather_fusion.3 = f32[2048]{0:T(1024)S(1)} fusion(f32[256,256]{1,0:T(8,128)S(1)} %add_divide_fusion, s32[2048]{0:T(1024)S(1)} %reshape.229), kind=kCustom, calls=%fused_computation.3 | custom fusion | bytes 32768 | tf_op jit(solution)/shard_map/jit(take_along_axis)/gather | solution.py:19
  132.8 0.1 reshape.232
  132.9 0.1 copy.36
  133.0 0.1 copy.37
  133.1 0.1 reshape.247
  133.3 8.2 %scatter_custom_fusion.1 = f32[129]{0:T(256)S(1)} fusion(s32[2048]{0:T(1024)S(1)} %bitcast.62, f32[2048]{0:T(1024)S(1)} %reshape.247, f32[]{:T(128)} %constant.24.clone.1), kind=kCustom, calls=%fused_computation.88 | custom fusion | bytes 520 | tf_op jit(solution)/shard_map/scatter | solution.py:40
  141.5 1.9 bitcast_multiply_fusion
  143.4 2.3 %scatter_custom_fusion.2 = f32[257,896]{1,0:T(8,128)S(1)} fusion(s32[128]{0:T(128)S(1)} %get-tuple-element.7, f32[128,896]{1,0:T(8,128)} %bitcast_multiply_fusion, f32[]{:T(128)} %constant.24.clone.1), kind=kCustom, calls=%fused_computation.31 | custom fusion | flops 114688 | bytes 921600 | tf_op jit(solution)/shard_map/scatter-add | solution.py:139
  145.7 1.9 reduce-scatter.3.cloned.1.call-done
  147.6 1.5 fusion.18
  149.1 0.8 copy-done.7
  149.9 1.3 fusion.23
  151.3 5.8 %psum.15 = f32[256]{0:T(256)S(1)} all-reduce(f32[256]{0:T(256)S(1)} %get-tuple-element.2), channel_id=1, replica_groups=mesh['ep'=8,'tp'=4] {'tp'}, use_global_device_ids=true, to_apply=%region_14.15 | all-reduce | flops 256 | bytes 2048 | tf_op jit(solution)/shard_map/psum | solution.py:151
  157.0 28.2 %all-reduce.3.cloned.1.call-done = f32[256,576]{0,1:T(8,128)} async-done(((f32[256,576]{0,1:T(8,128)}), f32[256,576]{0,1:T(8,128)}) %all-reduce.3.cloned.1.call-update) | async-done | bytes 589840 | tf_op jit(solution)/shard_map/psum | solution.py:151
  185.2 1.1 broadcast_multiply_fusion
  186.3 0.2 copy.38
  186.6 0.7 gather_fusion.1
  187.2 0.1 multiply_reduce_fusion
  187.4 0.2 fusion.43
  187.6 0.1 fusion.32
  187.7 0.7 pad_maximum_fusion
  (50 shorter events, 0.3 us)
Async XLA Ops:
  7.2 72.0 %copy-start = (bf16[256,3584]{1,0:T(8,128)(2,1)S(1)}, bf16[256,3584]{1,0:T(8,128)(2,1)}, u32[]{:S(2)}) copy-start(bf16[256,3584]{1,0:T(8,128)(2,1)} %param.21) | copy-start | bytes 5505028
  7.2 26.3 %all-gather.3.cloned.1.call-start = ((), (), s32[]{:S(2)}) async-start(), calls=%async_computation.4 | async-start | bytes 2293760 | tf_op jit(solution)/shard_map/all_gather | solution.py:102
  7.9 96.0 %reduce-scatter.5.cloned.1.call-start = ((), (), s32[]{:S(2)}) async-start(), calls=%async_computation.6 | async-start | bytes 2293760 | tf_op jit(solution)/shard_map/reduce_scatter | solution.py:136
  33.4 2.1 %copy-start.2 = (bf16[256,3584]{1,0:T(8,128)(2,1)S(1)}, bf16[256,3584]{1,0:T(8,128)(2,1)}, u32[]{:S(2)}) copy-start(bf16[256,3584]{1,0:T(8,128)(2,1)} %all-gather.3.cloned.1.call-done) | copy-start | bytes 5505028
  36.1 1.3 copy-start.1
  42.5 29.1 %copy-start.5 = (bf16[1,3584,256]{2,1,0:T(8,128)(2,1)S(1)}, bf16[1,3584,256]{2,1,0:T(8,128)(2,1)}, u32[]{:S(2)}) copy-start(bf16[1,3584,256]{2,1,0:T(8,128)(2,1)} %param.22) | copy-start | bytes 5505028
  71.7 1.5 copy-start.6
  73.2 1.5 copy-start.3
  76.4 71.2 %reduce-scatter.3.cloned.1.call-start = ((), (), s32[]{:S(2)}) async-start(), calls=%async_computation.5 | async-start | bytes 4587520 | tf_op jit(solution)/shard_map/reduce_scatter | solution.py:140
  85.2 0.7 copy-start.14
  85.2 0.8 copy-start.12
  85.2 0.8 copy-start.11
  85.2 0.8 copy-start.10
  85.2 1.1 copy-start.13
  85.2 3.3 %copy-start.9 = (bf16[896,256]{1,0:T(8,128)(2,1)S(1)}, bf16[896,256]{1,0:T(8,128)(2,1)}, u32[]{:S(2)}) copy-start(bf16[896,256]{1,0:T(8,128)(2,1)} %param.17) | copy-start | bytes 1376260
  103.9 37.6 %all-to-all-start.1 = ((f32[8,16,896]{2,1,0:T(8,128)}), f32[8,16,896]{2,1,0:T(8,128)}, u32[]{:S(2)}, u32[]{:S(2)}) async-start(f32[8,16,896]{2,1,0:T(8,128)} %reduce-scatter.5.cloned.1.call-done), calls=%async_computation.3 | async-start | bytes 917504 | tf_op jit(solution)/shard_map/all_to_all | solution.py:137
  109.4 75.8 %all-reduce.3.cloned.1.call-start = ((), (), s32[]{:S(2)}) async-start(), calls=%async_computation.7 | async-start | bytes 1179648 | tf_op jit(solution)/shard_map/psum | solution.py:151
  132.8 14.8 %copy-start.4 = (bf16[256,896]{1,0:T(8,128)(2,1)S(1)}, bf16[256,896]{1,0:T(8,128)(2,1)}, u32[]{:S(2)}) copy-start(bf16[256,896]{1,0:T(8,128)(2,1)} %param.15) | copy-start | bytes 1376260
  147.6 2.3 %copy-start.8 = (bf16[896,576]{0,1:T(8,128)(2,1)S(1)}, bf16[896,576]{0,1:T(8,128)(2,1)}, u32[]{:S(2)}) copy-start(bf16[896,576]{0,1:T(8,128)(2,1)} %param.26) | copy-start | bytes 3096580
  149.1 0.8 copy-start.7
Sparse Core Ops, SparseCore 0:
  9.6 23.8 all-gather.2
  76.5 27.3 reduce-scatter.4
  106.4 41.1 reduce-scatter.2
  151.4 33.8 all-reduce.2
